TPU v7x, 256 devices: a whole 4x4x8 slice. The times are simulated.
256 devices in a mesh: seq: 32 (over y, x, core), tensor: 8 (over z).
Axes of the slice: x: 4, y: 4, z: 8, core: 2. Of those that a mesh axis runs over, the one named last changes fastest.
Arguments:
- hidden: bfloat16 [8192, 3072], P('seq'), may hold values from -6 to 6
- attention_norm_gain: bfloat16 [3072], replicated, may hold values from 0.099609375 to 1.8984375
- query_key_value_weight: bfloat16 [3, 3072, 3072], P(None, None, 'tensor'), may hold values from -0.109375 to 0.109375
- output_weight: bfloat16 [3072, 3072], P('tensor'), may hold values from -0.3125 to 0.3125
- adapter_down_weight: bfloat16 [3072, 16], P('tensor'), may hold values from -0.3125 to 0.3125
- adapter_up_weight: bfloat16 [16, 3072], replicated, may hold values from -1.5 to 1.5
- final_norm_gain: bfloat16 [3072], replicated, may hold values from 0.099609375 to 1.8984375
- head: bfloat16 [16384, 3072], P('tensor', 'seq')
- prompt_key_slots: bfloat16 [64, 128, 3072], P('seq', None, 'tensor')
- prompt_value_slots: bfloat16 [64, 128, 3072], P('seq', None, 'tensor'), may hold values from -6 to 6
- counts: int32 [8], replicated, may hold values from 1 to 8, as said below
- page_slot_index: int32 [64], replicated, may hold values from 0 to 63, each once
- owner: int32 [128], replicated, may hold values from 0 to 7, as said below
- targets: int32 [8192], P('seq'), may hold values from 0 to 16383
Outputs:
- logprob_policy: float32 [8192], P('seq')
- logprob_reference: float32 [8192], P('seq')
Inputs may be any that keep to these rules, and one draw needn't show every extreme that they name: `counts`: every prompt fills 1 to 8 pages, and some prompt fills exactly 8. `page_slot_index`: slot s is held by index s // 2 of seq; every slot is named once. `owner`: every prompt owns exactly 16 rollouts, placed anywhere.
All inputs are finite; a program needn't handle non-finite values.
Results may differ from a plain program's by a relative error of at most 0.014.
The roundings to bfloat16 on the way count: a program that leaves them out, or rounds other values in their place, can miss the bound.
Values may be sent and summed in bfloat16 or wider, within the bound.
No kernel may reach another device: no remote copies, remote signals or barrier semaphores. Data moves between devices by JAX's collectives and lax.ppermute only.
A program may use at most 192 MiB of HBM per device.

v0:
```python
import math

import jax
import jax.numpy as jnp
from jax import lax
from jax.sharding import PartitionSpec as P

HEAD_WIDTH = 96
LEN = 64
PAGE = 128
MAXP = 8


EPSILON = 1e-05
NEGATIVE = -1e30


def rms_norm(values, gain):
    mean_sq = jnp.mean(values * values, axis=-1, keepdims=True)
    return (values * lax.rsqrt(mean_sq + EPSILON) * gain.astype(jnp.float32)).astype(jnp.bfloat16)


def rotate(values, positions):
    half_width = values.shape[-1] // 2
    frequency = 10000.0 ** (-jnp.arange(half_width, dtype=jnp.float32) * 2.0 / values.shape[-1])
    angles = positions.astype(jnp.float32)[:, None] * frequency[None, :]
    cosine = jnp.cos(angles)[:, None, :]
    sinus = jnp.sin(angles)[:, None, :]
    first = values[..., :half_width]
    second = values[..., half_width:]
    return jnp.concatenate(
        [first * cosine - second * sinus, second * cosine + first * sinus], axis=-1
    )


def local(
    hidden,
    attention_norm_gain,
    query_key_value_weight,
    output_weight,
    adapter_down_weight,
    adapter_up_weight,
    final_norm_gain,
    head,
    prompt_key_slots,
    prompt_value_slots,
    counts,
    page_slot_index,
    owner,
    targets,
):
    tok_rows = hidden.shape[0]
    rollouts_here = tok_rows // LEN
    heads_here = output_weight.shape[0] // HEAD_WIDTH
    width_here = heads_here * HEAD_WIDTH
    score_scale = 1.0 / math.sqrt(HEAD_WIDTH)
    stream = hidden.astype(jnp.float32)
    normed = rms_norm(stream, attention_norm_gain)
    groups_iota = jnp.arange(counts.shape[0], dtype=jnp.int32)
    my_groups = lax.dynamic_slice_in_dim(
        owner, lax.axis_index("seq") * rollouts_here, rollouts_here, 0
    )
    tok_group = jnp.repeat(my_groups, LEN)
    group_pages = jnp.sum(
        jnp.where(tok_group[:, None] == groups_iota[None, :], counts[None, :], 0), axis=1
    )
    positions = group_pages * PAGE + jnp.arange(tok_rows, dtype=jnp.int32) % LEN
    queries = rotate(
        jnp.dot(normed, query_key_value_weight[0], preferred_element_type=jnp.float32).reshape(
            tok_rows, heads_here, HEAD_WIDTH
        ),
        positions,
    ).astype(jnp.bfloat16)
    keys_new = rotate(
        jnp.dot(normed, query_key_value_weight[1], preferred_element_type=jnp.float32).reshape(
            tok_rows, heads_here, HEAD_WIDTH
        ),
        positions,
    ).astype(jnp.bfloat16)
    values_new = (
        jnp.dot(normed, query_key_value_weight[2], preferred_element_type=jnp.float32)
        .astype(jnp.bfloat16)
        .reshape(tok_rows, heads_here, HEAD_WIDTH)
    )
    query_roll = queries.reshape(rollouts_here, LEN, heads_here, HEAD_WIDTH)
    key_roll = keys_new.reshape(rollouts_here, LEN, heads_here, HEAD_WIDTH)
    value_roll = values_new.reshape(rollouts_here, LEN, heads_here, HEAD_WIDTH)
    causal = jnp.arange(LEN, dtype=jnp.int32)[None, :] <= jnp.arange(LEN, dtype=jnp.int32)[:, None]
    own_scores = (
        jnp.einsum("rthd,rkhd->rhtk", query_roll, key_roll, preferred_element_type=jnp.float32)
        * score_scale
    )
    own_max = jnp.max(jnp.where(causal, own_scores, NEGATIVE), axis=-1)
    own_weights = jnp.where(causal, jnp.exp(own_scores - own_max[..., None]), 0.0)
    own_total = jnp.sum(own_weights, axis=-1)
    own_summed = jnp.einsum(
        "rhtk,rkhd->rhtd",
        own_weights.astype(jnp.bfloat16),
        value_roll,
        preferred_element_type=jnp.float32,
    )
    start_max = jnp.transpose(own_max, (1, 0, 2)).reshape(heads_here, tok_rows)
    start_total = jnp.transpose(own_total, (1, 0, 2)).reshape(heads_here, tok_rows)
    start_summed = jnp.transpose(own_summed, (1, 0, 2, 3)).reshape(heads_here, tok_rows, HEAD_WIDTH)
    entries = jnp.arange(page_slot_index.shape[0], dtype=jnp.int32)
    key_piece = lax.all_gather(prompt_key_slots, "seq", axis=0, tiled=True)
    value_piece = lax.all_gather(prompt_value_slots, "seq", axis=0, tiled=True)
    piece_slots = key_piece.shape[0]
    slot_ids = jnp.arange(piece_slots, dtype=jnp.int32)
    matches = page_slot_index[None, :] == slot_ids[:, None]
    slot_group = jnp.sum(jnp.where(matches, entries // MAXP, 0), axis=1)
    slot_page = jnp.sum(jnp.where(matches, entries % MAXP, 0), axis=1)
    slot_count = jnp.sum(
        jnp.where(slot_group[:, None] == groups_iota[None, :], counts[None, :], 0), axis=1
    )
    key_live = jnp.repeat(slot_page < slot_count, PAGE)
    key_group = jnp.repeat(slot_group, PAGE)
    visible = (tok_group[:, None] == key_group[None, :]) & key_live[None, :]
    totals = start_total
    summed = start_summed
    keys_flat = key_piece.reshape(piece_slots * PAGE, heads_here, HEAD_WIDTH)
    values_flat = value_piece.reshape(piece_slots * PAGE, heads_here, HEAD_WIDTH)
    scores = (
        jnp.einsum("thd,khd->htk", queries, keys_flat, preferred_element_type=jnp.float32)
        * score_scale
    )
    block_max = jnp.max(jnp.where(visible[None], scores, NEGATIVE), axis=-1)
    new_max = jnp.maximum(start_max, block_max)
    weights = jnp.where(visible[None], jnp.exp(scores - new_max[..., None]), 0.0)
    rescale = jnp.exp(start_max - new_max)
    totals = totals * rescale + jnp.sum(weights, axis=-1)
    summed = summed * rescale[..., None] + jnp.einsum(
        "htk,khd->htd",
        weights.astype(jnp.bfloat16),
        values_flat,
        preferred_element_type=jnp.float32,
    )
    attention_output = (summed / totals[..., None]).astype(jnp.bfloat16)
    attention_output = jnp.transpose(attention_output, (1, 0, 2)).reshape(tok_rows, width_here)
    branch_part = jnp.dot(attention_output, output_weight, preferred_element_type=jnp.float32)
    adapter_portion = jnp.dot(
        attention_output, adapter_down_weight, preferred_element_type=jnp.float32
    )
    branch_sum, adapter_delta = (
        lax.psum(branch_part.astype(jnp.bfloat16), "tensor").astype(jnp.float32),
        lax.psum(adapter_portion.astype(jnp.bfloat16), "tensor").astype(jnp.float32),
    )
    reference_hidden = stream + branch_sum
    policy_hidden = reference_hidden + jnp.dot(
        adapter_delta, adapter_up_weight.astype(jnp.float32), precision=lax.Precision.HIGHEST
    )
    normed_ref = rms_norm(reference_hidden, final_norm_gain)
    normed_pol = rms_norm(policy_hidden, final_norm_gain)
    head_rows = lax.all_gather(head, "seq", axis=1, tiled=True)
    stacked = jnp.concatenate([normed_pol, normed_ref], axis=0)
    logits = lax.dot_general(
        stacked, head_rows, (((1,), (1,)), ((), ())), preferred_element_type=jnp.float32
    )
    vocab_here = head_rows.shape[0]
    target_ids = jnp.concatenate([targets, targets], axis=0) - lax.axis_index("tensor") * vocab_here
    is_target = jnp.arange(vocab_here, dtype=jnp.int32)[None, :] == target_ids[:, None]
    picked = jnp.sum(jnp.where(is_target, logits, 0.0), axis=1)
    local_max = jnp.max(logits, axis=1)
    whole_max = lax.pmax(local_max, "tensor")
    local_total = jnp.sum(jnp.exp(logits - whole_max[:, None]), axis=1)
    whole_total, whole_picked = lax.psum((local_total, picked), "tensor")
    log_probs = whole_picked - whole_max - jnp.log(whole_total)
    return (log_probs[:tok_rows], log_probs[tok_rows:])


def solution(mesh):
    return jax.shard_map(
        local,
        mesh=mesh,
        in_specs=(
            P("seq", None),
            P(),
            P(None, None, "tensor"),
            P("tensor", None),
            P("tensor", None),
            P(),
            P(),
            P("tensor", "seq"),
            P("seq", None, "tensor"),
            P("seq", None, "tensor"),
            P(),
            P(),
            P(),
            P("seq"),
        ),
        out_specs=(P("seq"), P("seq")),
        check_vma=False,
    )
```

profile of v0, /device:TPU:24, one launch (start us, length us, event | category | flops | bytes accessed | tf_op | source)
XLA Modules:
  0.0 395.7 jit_solution(10816526754883917571)
XLA Ops:
  8.0 0.7 all-gather.6.cloned.1.call-update
  8.7 0.7 dynamic_slice.3
  10.3 5.1 %slice_bitcast_fusion = (bf16[384,3072]{0,1:T(8,128)(2,1)}, bf16[384,3072]{0,1:T(8,128)(2,1)}) fusion(bf16[3,3072,384]{2,1,0:T(8,128)(2,1)} %param.16), kind=kLoop, calls=%fused_computation.29 | loop fusion | bytes 9437184 | tf_op jit(solution)/shard_map/dot_general | solution.py:75
  15.4 4.3 %copy.69 = bf16[384,3072]{1,0:T(8,128)(2,1)} copy(bf16[384,3072]{0,1:T(8,128)(2,1)} %get-tuple-element.10) | data formatting | bytes 4718592 | tf_op jit(solution)/shard_map/dot_general | solution.py:75
  19.7 4.3 %copy.66 = bf16[384,3072]{1,0:T(8,128)(2,1)} copy(bf16[384,3072]{0,1:T(8,128)(2,1)} %get-tuple-element.11) | data formatting | bytes 4718592 | tf_op jit(solution)/shard_map/dot_general | solution.py:69
  24.1 1.8 fusion.5
  26.2 3.2 fusion.15
  29.6 0.9 fusion.17
  31.5 0.9 copy.70
  32.5 0.9 copy.71
  33.4 1.5 select_reduce_fusion.2
  35.2 3.2 fusion.22
  39.5 2.8 compare_and_fusion
  42.3 24.3 %all-gather.4.cloned.1.call-done = bf16[64,128,384]{2,1,0:T(8,128)(2,1)} async-done(((bf16[2,128,384]{2,1,0:T(8,128)(2,1)}), bf16[64,128,384]{2,1,0:T(8,128)(2,1)}) %all-gather.4.cloned.1.call-update) | async-done | bytes 6291472 | tf_op jit(solution)/shard_map/all_gather | solution.py:106
  66.7 9.0 %copy.76 = bf16[64,128,384]{1,0,2:T(8,128)(2,1)} copy(bf16[64,128,384]{2,1,0:T(8,128)(2,1)} %all-gather.4.cloned.1.call-done) | data formatting | bytes 12582912 | tf_op jit(solution)/shard_map/all_gather | solution.py:106
  75.7 10.3 %reshape.235 = bf16[8192,4,96]{0,2,1:T(8,128)(2,1)} reshape(bf16[64,128,384]{1,0,2:T(8,128)(2,1)} %copy.76) | data formatting | bytes 12582912 | tf_op jit(solution)/shard_map/reshape | solution.py:121
  86.0 36.4 %all-gather.6.cloned.1.call-done = bf16[64,128,384]{2,1,0:T(8,128)(2,1)} async-done(((bf16[2,128,384]{2,1,0:T(8,128)(2,1)}), bf16[64,128,384]{2,1,0:T(8,128)(2,1)}) %all-gather.6.cloned.1.call-update) | async-done | bytes 6291472 | tf_op jit(solution)/shard_map/all_gather | solution.py:107
  122.4 9.1 %copy.78 = bf16[64,128,384]{1,0,2:T(8,128)(2,1)} copy(bf16[64,128,384]{2,1,0:T(8,128)(2,1)} %all-gather.6.cloned.1.call-done) | data formatting | bytes 12582912 | tf_op jit(solution)/shard_map/all_gather | solution.py:107
  131.5 10.3 %reshape.236 = bf16[8192,4,96]{0,2,1:T(8,128)(2,1)} reshape(bf16[64,128,384]{1,0,2:T(8,128)(2,1)} %copy.78) | data formatting | bytes 12582912 | tf_op jit(solution)/shard_map/reshape | solution.py:122
  141.8 18.0 %select_reduce_fusion = (f32[4,256]{1,0:T(4,128)S(1)}, f32[4,256,8192]{2,1,0:T(8,128)}) fusion(pred[256,8192]{1,0:T(8,128)(4,1)} %compare_and_fusion, bf16[8192,4,96]{0,2,1:T(8,128)(2,1)} %reshape.235, bf16[256,4,48]{0,2,1:T(8,128)(2,1)S(1)} %get-tuple-element.16, bf16[256,4,48]{0,2,1:T(8,128)(2,1)S(1)} %copy-done.7), kind=kOutput, calls=%fused_computation.1 | convolution fusion | flops 1636170752 | bytes 42143744 | tf_op jit(solution)/shard_map/thd,khd->htk/dot_general | solution.py:124
  159.8 15.2 %fusion = f32[4,256]{1,0:T(4,128)S(1)} fusion(f32[4,256,8192]{2,1,0:T(8,128)} %get-tuple-element.27, f32[4,256]{1,0:T(4,128)S(1)} %max.15, pred[256,8192]{1,0:T(8,128)(4,1)S(1)} %copy-done.4), kind=kLoop, calls=%fused_computation.2 | loop fusion | flops 33553408 | bytes 35659776 | tf_op jit(solution)/shard_map/reduce_sum | solution.py:131
  175.1 15.2 %fusion.28 = bf16[4,256,96]{1,2,0:T(8,128)(2,1)S(1)} fusion(bf16[8192,4,96]{0,2,1:T(8,128)(2,1)} %reshape.236, f32[4,256,8192]{2,1,0:T(8,128)} %get-tuple-element.27, f32[4,256]{1,0:T(4,128)S(1)} %max.15, pred[256,8192]{1,0:T(8,128)(4,1)S(1)} %copy-done.4, f32[4,256,96]{1,2,0:T(8,128)S(1)} %copy.77, f32[4,256]{1,0:T(4,128)S(1)} %get-tuple-element.8, ...), kind=kOutput, calls=%fused_computation.40 | convolution fusion | flops 1644560384 | bytes 42545152 | tf_op jit(solution)/shard_map/htk,khd->htd/dot_general | solution.py:132
  190.4 2.1 convolution_convert_fusion
  193.3 17.8 %psum.29 = bf16[256,16]{0,1:T(8,128)(2,1)S(1)} all-reduce(bf16[256,16]{0,1:T(8,128)(2,1)S(1)} %convolution_convert_fusion.1), channel_id=1, replica_groups=mesh['seq'=32,'tensor'=8] {'tensor'}, use_global_device_ids=true, to_apply=%region_10.11 | all-reduce | flops 4096 | bytes 16384 | tf_op jit(solution)/shard_map/psum | solution.py:146
  211.1 60.2 %all-reduce.3.cloned.1.call-done = bf16[256,3072]{1,0:T(8,128)(2,1)} async-done(((bf16[256,3072]{1,0:T(8,128)(2,1)}), bf16[256,3072]{1,0:T(8,128)(2,1)}) %all-reduce.3.cloned.1.call-update) | async-done | bytes 1572880 | tf_op jit(solution)/shard_map/psum | solution.py:145
  271.3 2.9 multiply_reduce_fusion.1
  274.8 3.0 multiply_convert_fusion.1
  277.8 62.8 %all-gather.8.cloned.1.call-done = bf16[2048,3072]{0,1:T(8,128)(2,1)} async-done(((bf16[2048,96]{0,1:T(8,128)(2,1)}), bf16[2048,3072]{0,1:T(8,128)(2,1)}) %all-gather.8.cloned.1.call-update) | async-done | bytes 12582928 | tf_op jit(solution)/shard_map/all_gather | solution.py:154
  340.6 11.9 %fusion.60 = (f32[512]{0:T(512)S(1)}, f32[512,2048]{1,0:T(8,128)}) fusion(bf16[2048,3072]{0,1:T(8,128)(2,1)} %all-gather.8.cloned.1.call-done, bf16[256,3072]{1,0:T(8,128)(2,1)} %get-tuple-element.19, bf16[256,3072]{1,0:T(8,128)(2,1)} %get-tuple-element.18), kind=kOutput, calls=%fused_computation.99 | convolution fusion | flops 6449790464 | bytes 19924992 | tf_op jit(solution)/shard_map/dot_general | solution.py:156
  352.5 17.4 %pmax.7 = f32[512]{0:T(512)S(1)} all-reduce(f32[512]{0:T(512)S(1)} %get-tuple-element.30), channel_id=1, replica_groups=mesh['seq'=32,'tensor'=8] {'tensor'}, use_global_device_ids=true, to_apply=%region_16.17 | all-reduce | flops 512 | bytes 4096 | tf_op jit(solution)/shard_map/pmax | solution.py:164
  369.9 3.6 select_reduce_fusion.1
  373.6 15.0 %all-reduce = (f32[512]{0:T(512)S(1)}, f32[512]{0:T(512)S(1)}) all-reduce(f32[512]{0:T(512)S(1)} %get-tuple-element.3, f32[512]{0:T(512)S(1)} %get-tuple-element.2), channel_id=1, replica_groups=mesh['seq'=32,'tensor'=8] {'tensor'}, use_global_device_ids=true, to_apply=%region_18.19 | all-reduce | flops 1024 | bytes 8192 | tf_op jit(solution)/shard_map/psum | solution.py:166
  (76 shorter events, 6.6 us)
Async XLA Ops:
  7.2 183.2 %copy-start = (bf16[384,3072]{1,0:T(8,128)(2,1)S(1)}, bf16[384,3072]{1,0:T(8,128)(2,1)}, u32[]{:S(2)}) copy-start(bf16[384,3072]{1,0:T(8,128)(2,1)} %param.17) | copy-start | bytes 7077892
  7.2 59.5 %all-gather.4.cloned.1.call-start = ((), (), s32[]{:S(2)}) async-start(), calls=%async_computation | async-start | bytes 6488064 | tf_op jit(solution)/shard_map/all_gather | solution.py:106
  7.9 114.5 %all-gather.6.cloned.1.call-start = ((), (), s32[]{:S(2)}) async-start(), calls=%async_computation.1 | async-start | bytes 6488064 | tf_op jit(solution)/shard_map/all_gather | solution.py:107
  8.7 262.7 %all-reduce.3.cloned.1.call-start = ((), (), s32[]{:S(2)}) async-start(), calls=%async_computation.2 | async-start | bytes 3145728 | tf_op jit(solution)/shard_map/psum | solution.py:145
  19.7 4.3 %copy-start.13 = (s32[8]{0:T(128)S(1)}, s32[8]{0:T(128)}, u32[]{:S(2)}) copy-start(s32[8]{0:T(128)} %param.24) | copy-start | bytes 100
  26.2 3.2 copy-start.1
  26.2 3.3 copy-start.5
  30.6 2.8 copy-start.6
  38.4 0.7 copy-start.12
  131.5 10.3 %copy-start.7 = (bf16[256,4,48]{0,2,1:T(8,128)(2,1)S(1)}, bf16[256,4,48]{0,2,1:T(8,128)(2,1)}, u32[]{:S(2)}) copy-start(bf16[256,4,48]{0,2,1:T(8,128)(2,1)} %copy-done.6) | copy-start | bytes 294916
  141.8 18.0 %copy-start.4 = (pred[256,8192]{1,0:T(8,128)(4,1)S(1)}, pred[256,8192]{1,0:T(8,128)(4,1)}, u32[]{:S(2)}) copy-start(pred[256,8192]{1,0:T(8,128)(4,1)} %compare_and_fusion) | copy-start | bytes 6291460
  190.3 2.8 copy-start.10
  190.3 2.8 copy-start.11
  190.3 2.8 copy-start.9
  190.4 81.0 %copy-start.8 = (bf16[16,3072]{1,0:T(8,128)(2,1)S(1)}, bf16[16,3072]{1,0:T(8,128)(2,1)}, u32[]{:S(2)}) copy-start(bf16[16,3072]{1,0:T(8,128)(2,1)} %param.19) | copy-start | bytes 294916
  192.5 148.1 %all-gather.8.cloned.1.call-start = ((), (), s32[]{:S(2)}) async-start(), calls=%async_computation.3 | async-start | bytes 12976128 | tf_op jit(solution)/shard_map/all_gather | solution.py:154
  271.3 2.9 copy-start.2
  271.3 2.9 copy-start.3
Sparse Core Ops, SparseCore 0:
  10.6 56.0 all-gather.3
  69.2 53.1 all-gather.5
  192.7 78.6 all-reduce.2
  273.7 66.8 all-gather.7
where the time goes:
time: 398 us; the launch traced here: 396 us
  waiting for transfers between devices  186 us (47%)
  matrix products  59.3 us (15%)
  local copies, waits for them, and re-layouts  57.6 us (14%)
  blocking collectives  50.3 us (13%)
  other arithmetic  28.7 us (7%)
  between operations  14.1 us (4%)
    all_gather x1, waiting for transfers between devices, local(): head_rows = lax.all_gather(head, 'seq', axis=1, tiled=True)  62.8 us
    psum x1, waiting for transfers between devices, local(): lax.psum(branch_part.astype(jnp.bfloat16), 'tensor').astype(jnp.float32)  60.2 us
    all_gather x1, waiting for transfers between devices, local(): value_piece = lax.all_gather(prompt_value_slots, 'seq', axis=0, tiled=True)  36.4 us
    all_gather x1, waiting for transfers between devices, local(): key_piece = lax.all_gather(prompt_key_slots, 'seq', axis=0, tiled=True)  24.3 us
    dot_general x1, matrix products, local(): jnp.einsum('thd,khd->htk', queries, keys_flat, preferred_element_type=jnp...  18 us
    psum x1, blocking collectives, local(): lax.psum(adapter_portion.astype(jnp.bfloat16), 'tensor').astype(jnp.float32)  17.8 us
    pmax x1, blocking collectives, local(): whole_max = lax.pmax(local_max, 'tensor')  17.4 us
    reduce_sum x1, other arithmetic, local(): totals = totals * rescale + jnp.sum(weights, axis=-1)  15.2 us
  transfers between devices with their start and end apart: 4, of which 4 were waited for; matrix products, arithmetic and copies ran while one was open for 15% of the time, Pallas kernels for 0%

commit v1 on v0

v1 whole, which is shorter than its diff:
```python
import math

import jax
import jax.numpy as jnp
from jax import lax
from jax.experimental import pallas as pl
from jax.experimental.pallas import tpu as pltpu
from jax.sharding import PartitionSpec as P

HEAD_WIDTH = 96
LEN = 64
PAGE = 128
MAXP = 8


EPSILON = 1e-05
NEGATIVE = -1e30
PAD = 128
VMEM_LIMIT = 56 * 1024 * 1024
F32 = jnp.float32
BF16 = jnp.bfloat16


def rms_norm(values, gain):
    mean_sq = jnp.mean(values * values, axis=-1, keepdims=True)
    return (values * lax.rsqrt(mean_sq + EPSILON) * gain.astype(F32)).astype(BF16)


def project_kernel(hidden_ref, gain_ref, weight_ref, cos_ref, sin_ref, out_ref, normed):
    part = pl.program_id(0)

    @pl.when(part == 0)
    def _():
        normed[...] = rms_norm(hidden_ref[...].astype(F32), gain_ref[...])

    product = jnp.dot(normed[...], weight_ref[0], preferred_element_type=F32)

    @pl.when(part < 2)
    def _():
        width = product.shape[1]
        half = HEAD_WIDTH // 2
        lane = lax.broadcasted_iota(jnp.int32, product.shape, 1) % HEAD_WIDTH
        partner = jnp.where(
            lane < half, -pltpu.roll(product, width - half, 1), pltpu.roll(product, half, 1)
        )
        out_ref[0] = (product * cos_ref[...] + partner * sin_ref[...]).astype(BF16)

    @pl.when(part == 2)
    def _():
        out_ref[0] = product.astype(BF16)


def project(hidden, gain, weight, cosine, sinus):
    rows, width = hidden.shape
    parts, _, cols = weight.shape
    whole = lambda i: (0, 0)
    return pl.pallas_call(
        project_kernel,
        grid=(parts,),
        in_specs=[
            pl.BlockSpec((rows, width), whole),
            pl.BlockSpec((1, width), whole),
            pl.BlockSpec((1, width, cols), lambda i: (i, 0, 0)),
            pl.BlockSpec((rows, cols), whole),
            pl.BlockSpec((rows, cols), whole),
        ],
        out_specs=pl.BlockSpec((1, rows, cols), lambda i: (i, 0, 0)),
        out_shape=jax.ShapeDtypeStruct((parts, rows, cols), BF16),
        scratch_shapes=[pltpu.VMEM((rows, width), BF16)],
        compiler_params=pltpu.CompilerParams(vmem_limit_bytes=VMEM_LIMIT),
        name="project",
    )(hidden, gain, weight, cosine, sinus)


def dot_nt(left, right):
    return lax.dot_general(left, right, (((1,), (1,)), ((), ())), preferred_element_type=F32)


def attend_kernel(
    first_ref,
    counts_ref,
    index_ref,
    owner_ref,
    qkv_ref,
    cache_ref,
    out_weight_ref,
    down_ref,
    out_ref,
    keys,
    values,
    attended,
    sems,
):
    rollouts = keys.shape[0]
    width = qkv_ref.shape[2]
    heads = width // HEAD_WIDTH
    scale = 1.0 / math.sqrt(HEAD_WIDTH)

    def copies(r, j):
        group = owner_ref[first_ref[0] + r]
        slot = index_ref[group * MAXP + j]
        rows = pl.ds(j * PAGE, PAGE)
        source = cache_ref.at[slot // 2]
        return (
            pltpu.make_async_copy(source.at[slot % 2], keys.at[r, rows], sems.at[r, 0, j]),
            pltpu.make_async_copy(source.at[2 + slot % 2], values.at[r, rows], sems.at[r, 1, j]),
        )

    for r in range(rollouts):
        for j in range(MAXP):
            for copy in copies(r, j):
                copy.start()
    lane_head = lax.broadcasted_iota(jnp.int32, (LEN, width), 1) // HEAD_WIDTH
    own_row = lax.broadcasted_iota(jnp.int32, (heads * LEN, LEN), 0) % LEN
    own_col = lax.broadcasted_iota(jnp.int32, (heads * LEN, LEN), 1)
    page_of = lax.broadcasted_iota(jnp.int32, (heads * LEN, MAXP * PAGE), 1) // PAGE
    for r in range(rollouts):
        rows = slice(r * LEN, (r + 1) * LEN)
        query = qkv_ref[0, rows, :].astype(F32)
        stacked = jnp.concatenate(
            [jnp.where(lane_head == h, query, 0.0) for h in range(heads)], axis=0
        ).astype(BF16)
        own = dot_nt(stacked, qkv_ref[1, rows, :]) * scale
        own = jnp.where(own_col <= own_row, own, NEGATIVE)
        for j in range(MAXP):
            for copy in copies(r, j):
                copy.wait()
        live = counts_ref[owner_ref[first_ref[0] + r]]
        cached = dot_nt(stacked, keys[r]) * scale
        cached = jnp.where(page_of < live, cached, NEGATIVE)
        largest = jnp.maximum(
            jnp.max(own, axis=1, keepdims=True), jnp.max(cached, axis=1, keepdims=True)
        )
        own = jnp.exp(own - largest)
        cached = jnp.exp(cached - largest)
        total = jnp.sum(own, axis=1, keepdims=True) + jnp.sum(cached, axis=1, keepdims=True)
        mixed = jnp.dot(cached.astype(BF16), values[r], preferred_element_type=F32) + jnp.dot(
            own.astype(BF16), qkv_ref[2, rows, :], preferred_element_type=F32
        )
        mixed = mixed / total
        picked = jnp.zeros((LEN, width), F32)
        for h in range(heads):
            picked = jnp.where(lane_head == h, mixed[h * LEN : (h + 1) * LEN], picked)
        attended[rows, :] = picked.astype(BF16)
    model = out_weight_ref.shape[1]
    out_ref[:, :model] = jnp.dot(
        attended[...], out_weight_ref[...], preferred_element_type=F32
    ).astype(BF16)
    out_ref[:, model:] = jnp.dot(
        attended[...], down_ref[...], preferred_element_type=F32
    ).astype(BF16)


def attend(first, counts, index, owner, qkv, cache, out_weight, down):
    _, rows, width = qkv.shape
    rollouts = rows // LEN
    model = out_weight.shape[1]
    vmem = pl.BlockSpec(memory_space=pltpu.VMEM)
    return pl.pallas_call(
        attend_kernel,
        grid_spec=pltpu.PrefetchScalarGridSpec(
            num_scalar_prefetch=4,
            grid=(),
            in_specs=[vmem, pl.BlockSpec(memory_space=pl.ANY), vmem, vmem],
            out_specs=vmem,
            scratch_shapes=[
                pltpu.VMEM((rollouts, MAXP * PAGE, width), BF16),
                pltpu.VMEM((rollouts, MAXP * PAGE, width), BF16),
                pltpu.VMEM((rows, width), BF16),
                pltpu.SemaphoreType.DMA((rollouts, 2, MAXP)),
            ],
        ),
        out_shape=jax.ShapeDtypeStruct((rows, model + PAD), BF16),
        compiler_params=pltpu.CompilerParams(vmem_limit_bytes=VMEM_LIMIT),
        name="attend",
    )(first, counts, index, owner, qkv, cache, out_weight, down)


def score_kernel(*refs):
    place_ref, hidden_ref, up_ref, gain_ref, target_ref, head_ref = refs[:6]
    out_ref, normed, largest, total, picked = refs[-5:]
    blocks = refs[6:-5]
    step = pl.program_id(0)
    ranks = len(blocks)
    model = hidden_ref.shape[1]
    rows = hidden_ref.shape[0]
    size = rows // ranks

    @pl.when(step == 0)
    def _():
        for k, block in enumerate(blocks):
            at = pl.ds(pl.multiple_of(place_ref[1 + k] * size, size), size)
            reference = hidden_ref[at, :].astype(F32) + block[:, :model].astype(F32)
            policy = reference + jnp.dot(
                block[:, model:], up_ref[...], preferred_element_type=F32
            )
            normed[0, at, :] = rms_norm(policy, gain_ref[...])
            normed[1, at, :] = rms_norm(reference, gain_ref[...])
        largest[...] = jnp.full_like(largest, NEGATIVE)
        total[...] = jnp.zeros_like(total)
        picked[...] = jnp.zeros_like(picked)

    logits = jnp.dot(
        normed[...].reshape(2 * rows, model), head_ref[...], preferred_element_type=F32
    )
    columns = lax.broadcasted_iota(jnp.int32, logits.shape, 1)
    wanted = target_ref[...] - (place_ref[0] * pl.num_programs(0) + step) * logits.shape[1]
    picked[...] += jnp.sum(jnp.where(columns == wanted, logits, 0.0), axis=1, keepdims=True)
    before = largest[...]
    after = jnp.maximum(before, jnp.max(logits, axis=1, keepdims=True))
    total[...] = total[...] * jnp.exp(before - after) + jnp.sum(
        jnp.exp(logits - after), axis=1, keepdims=True
    )
    largest[...] = after

    @pl.when(step == pl.num_programs(0) - 1)
    def _():
        lane = lax.broadcasted_iota(jnp.int32, (2 * rows, 128), 1)
        packed = jnp.where(
            lane == 0, largest[...], jnp.where(lane == 1, total[...], picked[...])
        )
        out_ref[...] = jnp.transpose(packed)[:8, :]


def score(place, hidden, up, gain, targets, head, blocks):
    rows, model = hidden.shape
    vocab = head.shape[1]
    tile = 512
    whole = lambda i, p: (0, 0)
    return pl.pallas_call(
        score_kernel,
        grid_spec=pltpu.PrefetchScalarGridSpec(
            num_scalar_prefetch=1,
            grid=(vocab // tile,),
            in_specs=[
                pl.BlockSpec(hidden.shape, whole),
                pl.BlockSpec(up.shape, whole),
                pl.BlockSpec(gain.shape, whole),
                pl.BlockSpec(targets.shape, whole),
                pl.BlockSpec((model, tile), lambda i, p: (0, i)),
            ]
            + [pl.BlockSpec(block.shape, whole) for block in blocks],
            out_specs=pl.BlockSpec((8, 2 * rows), whole),
            scratch_shapes=[
                pltpu.VMEM((2, rows, model), BF16),
                pltpu.VMEM((2 * rows, 1), F32),
                pltpu.VMEM((2 * rows, 1), F32),
                pltpu.VMEM((2 * rows, 1), F32),
            ],
        ),
        out_shape=jax.ShapeDtypeStruct((8, 2 * rows), F32),
        compiler_params=pltpu.CompilerParams(vmem_limit_bytes=VMEM_LIMIT),
        name="score",
    )(place, hidden, up, gain, targets, head, *blocks)


def shifted(value, ranks, step):
    return lax.ppermute(value, "tensor", [(i, (i + step) % ranks) for i in range(ranks)])


def ring_sum(branch, ranks):
    me = lax.axis_index("tensor")
    size = branch.shape[0] // ranks

    def mine(rank):
        return lax.dynamic_slice_in_dim(branch, (rank % ranks) * size, size, 0)

    half = ranks // 2
    left = mine(me + ranks - half)
    right = None
    for step in range(1, half + 1):
        arrived_left = shifted(left, ranks, -1)
        arrived_right = None if right is None else shifted(right, ranks, 1)
        if step == half:
            total = (
                mine(me).astype(F32) + arrived_left.astype(F32) + arrived_right.astype(F32)
            )
            return total.astype(BF16)
        left = (mine(me + ranks - half + step).astype(F32) + arrived_left.astype(F32)).astype(BF16)
        own = mine(me + half - step).astype(F32)
        if arrived_right is not None:
            own = own + arrived_right.astype(F32)
        right = own.astype(BF16)


def ring_gather(block, ranks):
    me = lax.axis_index("tensor")
    blocks, places = [block], [me]
    from_right = from_left = block
    for step in range(1, ranks // 2 + 1):
        from_right = shifted(from_right, ranks, -1)
        blocks.append(from_right)
        places.append((me + step) % ranks)
        if step < ranks // 2:
            from_left = shifted(from_left, ranks, 1)
            blocks.append(from_left)
            places.append((me + ranks - step) % ranks)
    return blocks, places


def local(
    hidden,
    attention_norm_gain,
    query_key_value_weight,
    output_weight,
    adapter_down_weight,
    adapter_up_weight,
    final_norm_gain,
    head,
    prompt_key_slots,
    prompt_value_slots,
    counts,
    page_slot_index,
    owner,
    targets,
):
    tok_rows, model = hidden.shape
    rollouts_here = tok_rows // LEN
    width_here = output_weight.shape[0]
    heads_here = width_here // HEAD_WIDTH
    ranks = lax.axis_size("tensor")
    first = lax.axis_index("seq") * rollouts_here
    cache = lax.all_gather(
        jnp.concatenate([prompt_key_slots, prompt_value_slots], axis=0)[None],
        "seq",
        axis=0,
        tiled=True,
    )
    head_columns = lax.all_gather(head.T, "seq", axis=0, tiled=True)

    groups_iota = jnp.arange(counts.shape[0], dtype=jnp.int32)
    my_groups = lax.dynamic_slice_in_dim(owner, first, rollouts_here, 0)
    my_pages = jnp.sum(
        jnp.where(my_groups[:, None] == groups_iota[None, :], counts[None, :], 0), axis=1
    )
    positions = jnp.repeat(my_pages, LEN) * PAGE + jnp.arange(tok_rows, dtype=jnp.int32) % LEN
    half = HEAD_WIDTH // 2
    place_in_head = jnp.arange(width_here, dtype=jnp.int32) % half
    frequency = 10000.0 ** (-place_in_head.astype(F32) * 2.0 / HEAD_WIDTH)
    angles = positions.astype(F32)[:, None] * frequency[None, :]
    qkv = project(
        hidden,
        attention_norm_gain[None, :],
        query_key_value_weight,
        jnp.cos(angles),
        jnp.sin(angles),
    )
    rank_pad = PAD - adapter_down_weight.shape[1]
    branch = attend(
        first[None].astype(jnp.int32),
        counts,
        page_slot_index,
        owner,
        qkv,
        cache,
        output_weight,
        jnp.pad(adapter_down_weight, ((0, 0), (0, rank_pad))),
    )
    blocks, places = ring_gather(ring_sum(branch, ranks), ranks)
    place = jnp.stack([lax.axis_index("tensor")] + places).astype(jnp.int32)
    stats = score(
        place,
        hidden,
        jnp.pad(adapter_up_weight, ((0, rank_pad), (0, 0))),
        final_norm_gain[None, :],
        jnp.concatenate([targets, targets])[:, None],
        head_columns,
        blocks,
    )
    every = jnp.stack([stats] + [shifted(stats, ranks, k) for k in range(1, ranks)])
    maxima, totals, picked = every[:, 0], every[:, 1], every[:, 2]
    largest = jnp.max(maxima, axis=0)
    total = jnp.sum(totals * jnp.exp(maxima - largest[None]), axis=0)
    log_probs = jnp.sum(picked, axis=0) - largest - jnp.log(total)
    return (log_probs[:tok_rows], log_probs[tok_rows:])


def solution(mesh):
    return jax.shard_map(
        local,
        mesh=mesh,
        in_specs=(
            P("seq", None),
            P(),
            P(None, None, "tensor"),
            P("tensor", None),
            P("tensor", None),
            P(),
            P(),
            P("tensor", "seq"),
            P("seq", None, "tensor"),
            P("seq", None, "tensor"),
            P(),
            P(),
            P(),
            P("seq"),
        ),
        out_specs=(P("seq"), P("seq")),
        check_vma=False,
    )
```

time: 398 us -> 209 us (0.53)
  waiting for transfers between devices: 186 us -> 98.4 us
  matrix products: 59.3 us -> 0 us
  blocking collectives: 50.3 us -> 0 us
  local copies, waits for them, and re-layouts: 57.6 us -> 8.41 us
  starting transfers between devices: 0.16 us -> 43.4 us
  Pallas kernels: 0 us -> 37 us
  other arithmetic: 28.7 us -> 6.65 us
    all_gather x3 -> x2, waiting for transfers between devices: 124 us -> 58.9 us  [the longest x1 58.9 us: local(): lax.all_gather(jnp.concatenate([prompt_key_slots, prompt_value_slots], ax...]
    psum x1 -> x0, waiting for transfers between devices: 60.2 us -> none  [local(): lax.psum(branch_part.astype(jnp.bfloat16), 'tensor').astype(jnp.float32)]
    dot_general x11 -> x0, matrix products: 59.3 us -> none  [the longest x1 18 us: local(): jnp.einsum('thd,khd->htk', queries, keys_flat, preferred_element_type=jnp...]
    ppermute x0 -> x21, starting transfers between devices: none -> 43.4 us  [shifted(): lax.ppermute(value, 'tensor', [(i, (i + step) % ranks) for i in range(ran...]
    ppermute x0 -> x21, waiting for transfers between devices: none -> 38.8 us  [shifted(): lax.ppermute(value, 'tensor', [(i, (i + step) % ranks) for i in range(ran...]
    pallas_call x0 -> x3, Pallas kernels: none -> 37 us  [the longest x1 17.9 us: score(): pl.pallas_call(score_kernel, grid_spec=pltpu.PrefetchScalarGridSpec(num_s...]
    psum x2 -> x0, blocking collectives: 32.8 us -> none  [the longest x1 17.8 us: local(): lax.psum(adapter_portion.astype(jnp.bfloat16), 'tensor').astype(jnp.float32)]
    reduce_sum x8 -> x3, other arithmetic: 21.7 us -> 0.26 us  [the longest x1 0.18 us: local(): jnp.sum(jnp.where(my_groups[:, None] == groups_iota[None, :], counts[None...]
  transfers between devices with their start and end apart: 4 -> 23, of which waited for: 4 -> 11; matrix products, arithmetic and copies ran while one was open for 15% -> 5% of each run, Pallas kernels for 0% -> 9%
where the time goes in v1:
time: 209 us; the launch traced here: 208 us
  waiting for transfers between devices  98.4 us (47%)
  starting transfers between devices  43.4 us (21%)
  Pallas kernels  37 us (18%)
  between operations  14.3 us (7%)
  local copies, waits for them, and re-layouts  8.41 us (4%)
  other arithmetic  6.65 us (3%)
    all_gather x1, waiting for transfers between devices, local(): lax.all_gather(jnp.concatenate([prompt_key_slots, prompt_value_slots], ax...  58.9 us
    ppermute x21, starting transfers between devices, shifted(): lax.ppermute(value, 'tensor', [(i, (i + step) % ranks) for i in range(ran...  43.4 us
    ppermute x21, waiting for transfers between devices, shifted(): lax.ppermute(value, 'tensor', [(i, (i + step) % ranks) for i in range(ran...  38.8 us
    pallas_call x1, Pallas kernels, score(): pl.pallas_call(score_kernel, grid_spec=pltpu.PrefetchScalarGridSpec(num_s...  17.9 us
    pallas_call x1, Pallas kernels, attend(): pl.pallas_call(attend_kernel, grid_spec=pltpu.PrefetchScalarGridSpec(num_...  11.2 us
    pallas_call x1, Pallas kernels, project(): pl.pallas_call(project_kernel, grid=(parts,), in_specs=[pl.BlockSpec((row...  7.94 us
  transfers between devices with their start and end apart: 23, of which 11 were waited for; matrix products, arithmetic and copies ran while one was open for 5% of the time, Pallas kernels for 9%

profile of v1, /device:TPU:24, one launch (start us, length us, event | category | flops | bytes accessed | tf_op | source)
XLA Modules:
  0.0 208.2 jit_solution(17469303197937097966)
XLA Ops:
  7.3 1.8 pad_maximum_fusion
  11.8 2.3 %multiply_sine_fusion = (f32[256,384]{1,0:T(8,128)}, f32[256,384]{1,0:T(8,128)}) fusion(f32[384]{0:T(512)S(1)} %fusion.7, f32[256]{0:T(256)S(1)} %fusion.12), kind=kLoop, calls=%fused_computation | loop fusion | flops 98304 | bytes 788992 | tf_op jit(solution)/shard_map/sin | solution.py:346
  14.1 7.9 %project.1.qkv_ref = bf16[3,256,384]{2,1,0:T(8,128)(2,1)} custom-call(bf16[256,3072]{1,0:T(8,128)(2,1)} %refs_1_.1, bf16[1,3072]{1,0:T(2,128)(2,1)} %broadcast_in_dim.39.gain_ref, bf16[3,3072,384]{2,1,0:T(8,128)(2,1)} %weight_ref.1, f32[256,384]{1,0:T(8,128)} %get-tuple-element.11.cos_ref, f32[256,384]{1,0:T(8,128)} %get-tuple-element.10.sin_ref), custom_call_target="tpu_custom_call" | custom-call | tf_op jit(solution)/shard_map/project/pallas_call | solution.py:57
  22.0 58.9 %all-gather.6.cloned.1.call-done = bf16[128,128,384]{2,1,0:T(8,128)(2,1)} async-done(((bf16[4,128,384]{2,1,0:T(8,128)(2,1)}), bf16[128,128,384]{2,1,0:T(8,128)(2,1)}) %all-gather.6.cloned.1.call-update) | async-done | bytes 12582928 | tf_op jit(solution)/shard_map/all_gather | solution.py:323
  80.9 11.2 %attend.1 = bf16[256,3200]{1,0:T(8,128)(2,1)} custom-call(s32[1]{0:T(128)} %bitcast.10.first_ref, s32[8]{0:T(128)} %counts_ref.1, s32[64]{0:T(128)} %index_ref.1, s32[128]{0:T(128)} %owner_ref.1, bf16[3,256,384]{2,1,0:T(8,128)(2,1)} %project.1.qkv_ref, bf16[32,4,128,384]{3,2,1,0:T(8,128)(2,1)} %bitcast.40, bf16[384,3072]{1,0:T(8,128)(2,1)} %out_weight_ref.1, ...), custom_call_target="tpu_custom_call" | custom-call | tf_op jit(solution)/shard_map/attend/pallas_call | solution.py:159
  92.1 1.2 constant_dynamic-slice_fusion.1
  93.3 3.4 %collective-permute-start = (bf16[32,3200]{1,0:T(8,128)(2,1)S(1)}, bf16[32,3200]{1,0:T(8,128)(2,1)S(1)}, u32[]{:S(2)}, u32[]{:S(2)}) collective-permute-start(bf16[32,3200]{1,0:T(8,128)(2,1)S(1)} %get-tuple-element.6), channel_id=1, source_target_pairs={{0,7},{1,0},{2,1},{3,2},{4,3},{5,4},{6,5},{7,6},{8,15},{9,8},{10,9... | collective-permute-start | bytes 614408 | tf_op jit(solution)/shard_map/ppermute | solution.py:258
  96.7 4.8 %collective-permute-done = bf16[32,3200]{1,0:T(8,128)(2,1)S(1)} collective-permute-done((bf16[32,3200]{1,0:T(8,128)(2,1)S(1)}, bf16[32,3200]{1,0:T(8,128)(2,1)S(1)}, u32[]{:S(2)}, u32[]{:S(2)}) %collective-permute-start) | collective-permute-done | bytes 204832 | tf_op jit(solution)/shard_map/ppermute | solution.py:258
  101.5 1.0 add_convert_fusion.5
  102.4 3.8 %collective-permute-start.1 = (bf16[32,3200]{1,0:T(8,128)(2,1)S(1)}, bf16[32,3200]{1,0:T(8,128)(2,1)S(1)}, u32[]{:S(2)}, u32[]{:S(2)}) collective-permute-start(bf16[32,3200]{1,0:T(8,128)(2,1)S(1)} %add_convert_fusion.5), channel_id=1, source_target_pairs={{0,7},{1,0},{2,1},{3,2},{4,3},{5,4},{6,5},{7,6},{8,15},{9,8},{10,9... | collective-permute-start | bytes 614408 | tf_op jit(solution)/shard_map/ppermute | solution.py:258
  106.2 4.0 %collective-permute-done.1 = bf16[32,3200]{1,0:T(8,128)(2,1)S(1)} collective-permute-done((bf16[32,3200]{1,0:T(8,128)(2,1)S(1)}, bf16[32,3200]{1,0:T(8,128)(2,1)S(1)}, u32[]{:S(2)}, u32[]{:S(2)}) %collective-permute-start.1) | collective-permute-done | bytes 204832 | tf_op jit(solution)/shard_map/ppermute | solution.py:258
  110.3 1.0 add_convert_fusion.4
  111.3 3.9 %collective-permute-start.2 = (bf16[32,3200]{1,0:T(8,128)(2,1)S(1)}, bf16[32,3200]{1,0:T(8,128)(2,1)S(1)}, u32[]{:S(2)}, u32[]{:S(2)}) collective-permute-start(bf16[32,3200]{1,0:T(8,128)(2,1)S(1)} %add_convert_fusion.4), channel_id=1, source_target_pairs={{0,7},{1,0},{2,1},{3,2},{4,3},{5,4},{6,5},{7,6},{8,15},{9,8},{10,9... | collective-permute-start | bytes 614408 | tf_op jit(solution)/shard_map/ppermute | solution.py:258
  115.2 3.3 %collective-permute-done.2 = bf16[32,3200]{1,0:T(8,128)(2,1)S(1)} collective-permute-done((bf16[32,3200]{1,0:T(8,128)(2,1)S(1)}, bf16[32,3200]{1,0:T(8,128)(2,1)S(1)}, u32[]{:S(2)}, u32[]{:S(2)}) %collective-permute-start.2) | collective-permute-done | bytes 204832 | tf_op jit(solution)/shard_map/ppermute | solution.py:258
  118.7 3.8 %collective-permute-start.3 = (bf16[32,3200]{1,0:T(8,128)(2,1)S(1)}, bf16[32,3200]{1,0:T(8,128)(2,1)S(1)}, u32[]{:S(2)}, u32[]{:S(2)}) collective-permute-start(bf16[32,3200]{1,0:T(8,128)(2,1)S(1)} %get-tuple-element.4), channel_id=1, source_target_pairs={{0,7},{1,0},{2,1},{3,2},{4,3},{5,4},{6,5},{7,6},{8,15},{9,8},{10,9... | collective-permute-start | bytes 614408 | tf_op jit(solution)/shard_map/ppermute | solution.py:258
  122.5 3.6 %collective-permute-done.5 = bf16[32,3200]{1,0:T(8,128)(2,1)S(1)} collective-permute-done((bf16[32,3200]{1,0:T(8,128)(2,1)S(1)}, bf16[32,3200]{1,0:T(8,128)(2,1)S(1)}, u32[]{:S(2)}, u32[]{:S(2)}) %collective-permute-start.5) | collective-permute-done | bytes 204832 | tf_op jit(solution)/shard_map/ppermute | solution.py:258
  126.3 6.9 %collective-permute-done.6 = bf16[32,3200]{1,0:T(8,128)(2,1)S(1)} collective-permute-done((bf16[32,3200]{1,0:T(8,128)(2,1)S(1)}, bf16[32,3200]{1,0:T(8,128)(2,1)S(1)}, u32[]{:S(2)}, u32[]{:S(2)}) %collective-permute-start.6) | collective-permute-done | bytes 204832 | tf_op jit(solution)/shard_map/ppermute | solution.py:258
  133.3 3.1 %collective-permute-start.7 = (bf16[32,3200]{1,0:T(8,128)(2,1)S(1)}, bf16[32,3200]{1,0:T(8,128)(2,1)S(1)}, u32[]{:S(2)}, u32[]{:S(2)}) collective-permute-start(bf16[32,3200]{1,0:T(8,128)(2,1)S(1)} %add_convert_fusion.refs_6_), channel_id=1, source_target_pairs={{0,7},{1,0},{2,1},{3,2},{4,3},{5,4},{6,5},{7,6},{8,15},{9,8},{10,9... | collective-permute-start | bytes 614408 | tf_op jit(solution)/shard_map/ppermute | solution.py:258
  136.4 5.0 %collective-permute-done.7.refs_7_ = bf16[32,3200]{1,0:T(8,128)(2,1)S(1)} collective-permute-done((bf16[32,3200]{1,0:T(8,128)(2,1)S(1)}, bf16[32,3200]{1,0:T(8,128)(2,1)S(1)}, u32[]{:S(2)}, u32[]{:S(2)}) %collective-permute-start.7) | collective-permute-done | bytes 204832 | tf_op jit(solution)/shard_map/ppermute | solution.py:258
  141.4 3.7 %collective-permute-start.9 = (bf16[32,3200]{1,0:T(8,128)(2,1)S(1)}, bf16[32,3200]{1,0:T(8,128)(2,1)S(1)}, u32[]{:S(2)}, u32[]{:S(2)}) collective-permute-start(bf16[32,3200]{1,0:T(8,128)(2,1)S(1)} %collective-permute-done.7.refs_7_), channel_id=1, source_target_pairs={{0,7},{1,0},{2,1},{3,2},{4,3},{5,4},{6,5},{7,6},{8,15},{9,8},{10,9... | collective-permute-start | bytes 614408 | tf_op jit(solution)/shard_map/ppermute | solution.py:258
  145.1 4.4 %collective-permute-done.9.refs_9_ = bf16[32,3200]{1,0:T(8,128)(2,1)S(1)} collective-permute-done((bf16[32,3200]{1,0:T(8,128)(2,1)S(1)}, bf16[32,3200]{1,0:T(8,128)(2,1)S(1)}, u32[]{:S(2)}, u32[]{:S(2)}) %collective-permute-start.9) | collective-permute-done | bytes 204832 | tf_op jit(solution)/shard_map/ppermute | solution.py:258
  149.5 3.7 %collective-permute-start.11 = (bf16[32,3200]{1,0:T(8,128)(2,1)S(1)}, bf16[32,3200]{1,0:T(8,128)(2,1)S(1)}, u32[]{:S(2)}, u32[]{:S(2)}) collective-permute-start(bf16[32,3200]{1,0:T(8,128)(2,1)S(1)} %collective-permute-done.9.refs_9_), channel_id=1, source_target_pairs={{0,7},{1,0},{2,1},{3,2},{4,3},{5,4},{6,5},{7,6},{8,15},{9,8},{10,9... | collective-permute-start | bytes 614408 | tf_op jit(solution)/shard_map/ppermute | solution.py:258
  153.2 3.6 %collective-permute-done.11.refs_11_ = bf16[32,3200]{1,0:T(8,128)(2,1)S(1)} collective-permute-done((bf16[32,3200]{1,0:T(8,128)(2,1)S(1)}, bf16[32,3200]{1,0:T(8,128)(2,1)S(1)}, u32[]{:S(2)}, u32[]{:S(2)}) %collective-permute-start.11) | collective-permute-done | bytes 204832 | tf_op jit(solution)/shard_map/ppermute | solution.py:258
  156.8 3.7 %collective-permute-start.13 = (bf16[32,3200]{1,0:T(8,128)(2,1)S(1)}, bf16[32,3200]{1,0:T(8,128)(2,1)S(1)}, u32[]{:S(2)}, u32[]{:S(2)}) collective-permute-start(bf16[32,3200]{1,0:T(8,128)(2,1)S(1)} %collective-permute-done.11.refs_11_), channel_id=1, source_target_pairs={{0,7},{1,0},{2,1},{3,2},{4,3},{5,4},{6,5},{7,6},{8,15},{9,8},{10,9... | collective-permute-start | bytes 614408 | tf_op jit(solution)/shard_map/ppermute | solution.py:258
  160.5 1.0 pad.8.refs_2_
  161.5 0.9 copy.25.refs_4_
  164.9 17.9 %score.1 = f32[8,512]{1,0:T(8,128)} custom-call(s32[9]{0:T(128)} %stack.63.refs_0_, bf16[256,3072]{1,0:T(8,128)(2,1)} %refs_1_.1, bf16[128,3072]{1,0:T(8,128)(2,1)} %pad.8.refs_2_, bf16[1,3072]{1,0:T(2,128)(2,1)} %broadcast_in_dim.36.refs_3_, s32[512,1]{1,0:T(8,128)} %copy.25.refs_4_, bf16[3072,2048]{1,0:T(8,128)(2,1)} %all-gather.4.cloned.1.call-done.refs_5_, ...), custom_call_target="tpu_custom_call" | custom-call | tf_op jit(solution)/shard_map/score/pallas_call | solution.py:230
  183.5 4.0 %collective-permute-start.15 = (f32[8,512]{1,0:T(8,128)}, f32[8,512]{1,0:T(8,128)S(1)}, u32[]{:S(2)}, u32[]{:S(2)}) collective-permute-start(f32[8,512]{1,0:T(8,128)} %score.1), channel_id=1, source_target_pairs={{0,2},{1,3},{2,4},{3,5},{4,6},{5,7},{6,0},{7,1},{8,10},{9,11},{10,... | collective-permute-start | bytes 49160 | tf_op jit(solution)/shard_map/ppermute | solution.py:258
  187.9 2.9 %collective-permute-start.17 = (f32[8,512]{1,0:T(8,128)}, f32[8,512]{1,0:T(8,128)S(1)}, u32[]{:S(2)}, u32[]{:S(2)}) collective-permute-start(f32[8,512]{1,0:T(8,128)} %score.1), channel_id=1, source_target_pairs={{0,4},{1,5},{2,6},{3,7},{4,0},{5,1},{6,2},{7,3},{8,12},{9,13},{10,... | collective-permute-start | bytes 49160 | tf_op jit(solution)/shard_map/ppermute | solution.py:258
  190.9 4.8 %collective-permute-start.18 = (f32[8,512]{1,0:T(8,128)}, f32[8,512]{1,0:T(8,128)S(1)}, u32[]{:S(2)}, u32[]{:S(2)}) collective-permute-start(f32[8,512]{1,0:T(8,128)} %score.1), channel_id=1, source_target_pairs={{0,5},{1,6},{2,7},{3,0},{4,1},{5,2},{6,3},{7,4},{8,13},{9,14},{10,... | collective-permute-start | bytes 49160 | tf_op jit(solution)/shard_map/ppermute | solution.py:258
  196.2 1.5 collective-permute-start.20
  197.7 2.9 %collective-permute-done.19 = f32[8,512]{1,0:T(8,128)S(1)} collective-permute-done((f32[8,512]{1,0:T(8,128)}, f32[8,512]{1,0:T(8,128)S(1)}, u32[]{:S(2)}, u32[]{:S(2)}) %collective-permute-start.19) | collective-permute-done | bytes 16416 | tf_op jit(solution)/shard_map/ppermute | solution.py:258
  (86 shorter events, 8.0 us)
Async XLA Ops:
  7.2 73.7 %all-gather.6.cloned.1.call-start = ((), (), s32[]{:S(2)}) async-start(), calls=%async_computation.1 | async-start | bytes 12976128 | tf_op jit(solution)/shard_map/all_gather | solution.py:323
  9.1 154.4 %all-gather.4.cloned.1.call-start = ((), (), s32[]{:S(2)}) async-start(), calls=%async_computation | async-start | bytes 12976128 | tf_op jit(solution)/shard_map/all_gather | solution.py:329
  92.1 26.4 %copy-start = (bf16[256,3200]{1,0:T(8,128)(2,1)S(1)}, bf16[256,3200]{1,0:T(8,128)(2,1)}, u32[]{:S(2)}) copy-start(bf16[256,3200]{1,0:T(8,128)(2,1)} %attend.1) | copy-start | bytes 4915204
  93.3 8.1 %collective-permute-start = (bf16[32,3200]{1,0:T(8,128)(2,1)S(1)}, bf16[32,3200]{1,0:T(8,128)(2,1)S(1)}, u32[]{:S(2)}, u32[]{:S(2)}) collective-permute-start(bf16[32,3200]{1,0:T(8,128)(2,1)S(1)} %get-tuple-element.6), channel_id=1, source_target_pairs={{0,7},{1,0},{2,1},{3,2},{4,3},{5,4},{6,5},{7,6},{8,15},{9,8},{10,9... | collective-permute-start | bytes 614408 | tf_op jit(solution)/shard_map/ppermute | solution.py:258
  102.4 7.8 %collective-permute-start.1 = (bf16[32,3200]{1,0:T(8,128)(2,1)S(1)}, bf16[32,3200]{1,0:T(8,128)(2,1)S(1)}, u32[]{:S(2)}, u32[]{:S(2)}) collective-permute-start(bf16[32,3200]{1,0:T(8,128)(2,1)S(1)} %add_convert_fusion.5), channel_id=1, source_target_pairs={{0,7},{1,0},{2,1},{3,2},{4,3},{5,4},{6,5},{7,6},{8,15},{9,8},{10,9... | collective-permute-start | bytes 614408 | tf_op jit(solution)/shard_map/ppermute | solution.py:258
  106.2 54.3 %copy-start.9 = (bf16[16,3072]{1,0:T(8,128)(2,1)S(1)}, bf16[16,3072]{1,0:T(8,128)(2,1)}, u32[]{:S(2)}) copy-start(bf16[16,3072]{1,0:T(8,128)(2,1)} %param.19) | copy-start | bytes 294916
  106.2 9.0 %collective-permute-start.4 = (bf16[32,3200]{1,0:T(8,128)(2,1)S(1)}, bf16[32,3200]{1,0:T(8,128)(2,1)S(1)}, u32[]{:S(2)}, u32[]{:S(2)}) collective-permute-start(bf16[32,3200]{1,0:T(8,128)(2,1)S(1)} %get-tuple-element.7), channel_id=1, source_target_pairs={{0,1},{1,2},{2,3},{3,4},{4,5},{5,6},{6,7},{7,0},{8,9},{9,10},{10,1... | collective-permute-start | bytes 614408 | tf_op jit(solution)/shard_map/ppermute | solution.py:258
  111.3 7.2 %collective-permute-start.2 = (bf16[32,3200]{1,0:T(8,128)(2,1)S(1)}, bf16[32,3200]{1,0:T(8,128)(2,1)S(1)}, u32[]{:S(2)}, u32[]{:S(2)}) collective-permute-start(bf16[32,3200]{1,0:T(8,128)(2,1)S(1)} %add_convert_fusion.4), channel_id=1, source_target_pairs={{0,7},{1,0},{2,1},{3,2},{4,3},{5,4},{6,5},{7,6},{8,15},{9,8},{10,9... | collective-permute-start | bytes 614408 | tf_op jit(solution)/shard_map/ppermute | solution.py:258
  115.2 46.3 %copy-start.13 = (s32[256]{0:T(256)S(1)}, s32[256]{0:T(256)}, u32[]{:S(2)}) copy-start(s32[256]{0:T(256)} %param.27) | copy-start | bytes 3076
  115.2 47.1 %copy-start.12 = (bf16[3072]{0:T(1024)(128)(2,1)S(1)}, bf16[3072]{0:T(1024)(128)(2,1)}, u32[]{:S(2)}) copy-start(bf16[3072]{0:T(1024)(128)(2,1)} %param.20) | copy-start | bytes 18436
  118.6 7.5 %collective-permute-start.5 = (bf16[32,3200]{1,0:T(8,128)(2,1)S(1)}, bf16[32,3200]{1,0:T(8,128)(2,1)S(1)}, u32[]{:S(2)}, u32[]{:S(2)}) collective-permute-start(bf16[32,3200]{1,0:T(8,128)(2,1)S(1)} %get-tuple-element.5), channel_id=1, source_target_pairs={{0,1},{1,2},{2,3},{3,4},{4,5},{5,6},{6,7},{7,0},{8,9},{9,10},{10,1... | collective-permute-start | bytes 614408 | tf_op jit(solution)/shard_map/ppermute | solution.py:258
  118.7 7.6 %collective-permute-start.3 = (bf16[32,3200]{1,0:T(8,128)(2,1)S(1)}, bf16[32,3200]{1,0:T(8,128)(2,1)S(1)}, u32[]{:S(2)}, u32[]{:S(2)}) collective-permute-start(bf16[32,3200]{1,0:T(8,128)(2,1)S(1)} %get-tuple-element.4), channel_id=1, source_target_pairs={{0,7},{1,0},{2,1},{3,2},{4,3},{5,4},{6,5},{7,6},{8,15},{9,8},{10,9... | collective-permute-start | bytes 614408 | tf_op jit(solution)/shard_map/ppermute | solution.py:258
  126.2 7.0 %collective-permute-start.6 = (bf16[32,3200]{1,0:T(8,128)(2,1)S(1)}, bf16[32,3200]{1,0:T(8,128)(2,1)S(1)}, u32[]{:S(2)}, u32[]{:S(2)}) collective-permute-start(bf16[32,3200]{1,0:T(8,128)(2,1)S(1)} %add_convert_fusion.1), channel_id=1, source_target_pairs={{0,1},{1,2},{2,3},{3,4},{4,5},{5,6},{6,7},{7,0},{8,9},{9,10},{10,1... | collective-permute-start | bytes 614408 | tf_op jit(solution)/shard_map/ppermute | solution.py:258
  133.3 30.5 %copy-start.1 = (bf16[32,3200]{1,0:T(8,128)(2,1)}, bf16[32,3200]{1,0:T(8,128)(2,1)S(1)}, u32[]{:S(2)}) copy-start(bf16[32,3200]{1,0:T(8,128)(2,1)S(1)} %add_convert_fusion.refs_6_) | copy-start | bytes 614404
  133.3 8.1 %collective-permute-start.7 = (bf16[32,3200]{1,0:T(8,128)(2,1)S(1)}, bf16[32,3200]{1,0:T(8,128)(2,1)S(1)}, u32[]{:S(2)}, u32[]{:S(2)}) collective-permute-start(bf16[32,3200]{1,0:T(8,128)(2,1)S(1)} %add_convert_fusion.refs_6_), channel_id=1, source_target_pairs={{0,7},{1,0},{2,1},{3,2},{4,3},{5,4},{6,5},{7,6},{8,15},{9,8},{10,9... | collective-permute-start | bytes 614408 | tf_op jit(solution)/shard_map/ppermute | solution.py:258
  136.4 8.7 %collective-permute-start.8 = (bf16[32,3200]{1,0:T(8,128)(2,1)S(1)}, bf16[32,3200]{1,0:T(8,128)(2,1)S(1)}, u32[]{:S(2)}, u32[]{:S(2)}) collective-permute-start(bf16[32,3200]{1,0:T(8,128)(2,1)S(1)} %add_convert_fusion.refs_6_), channel_id=1, source_target_pairs={{0,1},{1,2},{2,3},{3,4},{4,5},{5,6},{6,7},{7,0},{8,9},{9,10},{10,1... | collective-permute-start | bytes 614408 | tf_op jit(solution)/shard_map/ppermute | solution.py:258
  141.4 22.3 %copy-start.2 = (bf16[32,3200]{1,0:T(8,128)(2,1)}, bf16[32,3200]{1,0:T(8,128)(2,1)S(1)}, u32[]{:S(2)}) copy-start(bf16[32,3200]{1,0:T(8,128)(2,1)S(1)} %collective-permute-done.7.refs_7_) | copy-start | bytes 614404
  141.4 8.1 %collective-permute-start.9 = (bf16[32,3200]{1,0:T(8,128)(2,1)S(1)}, bf16[32,3200]{1,0:T(8,128)(2,1)S(1)}, u32[]{:S(2)}, u32[]{:S(2)}) collective-permute-start(bf16[32,3200]{1,0:T(8,128)(2,1)S(1)} %collective-permute-done.7.refs_7_), channel_id=1, source_target_pairs={{0,7},{1,0},{2,1},{3,2},{4,3},{5,4},{6,5},{7,6},{8,15},{9,8},{10,9... | collective-permute-start | bytes 614408 | tf_op jit(solution)/shard_map/ppermute | solution.py:258
  145.1 18.6 %copy-start.3 = (bf16[32,3200]{1,0:T(8,128)(2,1)}, bf16[32,3200]{1,0:T(8,128)(2,1)S(1)}, u32[]{:S(2)}) copy-start(bf16[32,3200]{1,0:T(8,128)(2,1)S(1)} %collective-permute-done.8.refs_8_) | copy-start | bytes 614404
  145.1 8.1 %collective-permute-start.10 = (bf16[32,3200]{1,0:T(8,128)(2,1)S(1)}, bf16[32,3200]{1,0:T(8,128)(2,1)S(1)}, u32[]{:S(2)}, u32[]{:S(2)}) collective-permute-start(bf16[32,3200]{1,0:T(8,128)(2,1)S(1)} %collective-permute-done.8.refs_8_), channel_id=1, source_target_pairs={{0,1},{1,2},{2,3},{3,4},{4,5},{5,6},{6,7},{7,0},{8,9},{9,10},{10,1... | collective-permute-start | bytes 614408 | tf_op jit(solution)/shard_map/ppermute | solution.py:258
  149.5 14.3 %copy-start.4 = (bf16[32,3200]{1,0:T(8,128)(2,1)}, bf16[32,3200]{1,0:T(8,128)(2,1)S(1)}, u32[]{:S(2)}) copy-start(bf16[32,3200]{1,0:T(8,128)(2,1)S(1)} %collective-permute-done.9.refs_9_) | copy-start | bytes 614404
  149.5 7.3 %collective-permute-start.11 = (bf16[32,3200]{1,0:T(8,128)(2,1)S(1)}, bf16[32,3200]{1,0:T(8,128)(2,1)S(1)}, u32[]{:S(2)}, u32[]{:S(2)}) collective-permute-start(bf16[32,3200]{1,0:T(8,128)(2,1)S(1)} %collective-permute-done.9.refs_9_), channel_id=1, source_target_pairs={{0,7},{1,0},{2,1},{3,2},{4,3},{5,4},{6,5},{7,6},{8,15},{9,8},{10,9... | collective-permute-start | bytes 614408 | tf_op jit(solution)/shard_map/ppermute | solution.py:258
  153.2 10.6 %copy-start.5 = (bf16[32,3200]{1,0:T(8,128)(2,1)}, bf16[32,3200]{1,0:T(8,128)(2,1)S(1)}, u32[]{:S(2)}) copy-start(bf16[32,3200]{1,0:T(8,128)(2,1)S(1)} %collective-permute-done.10.refs_10_) | copy-start | bytes 614404
  153.2 10.4 %collective-permute-start.12 = (bf16[32,3200]{1,0:T(8,128)(2,1)S(1)}, bf16[32,3200]{1,0:T(8,128)(2,1)S(1)}, u32[]{:S(2)}, u32[]{:S(2)}) collective-permute-start(bf16[32,3200]{1,0:T(8,128)(2,1)S(1)} %collective-permute-done.10.refs_10_), channel_id=1, source_target_pairs={{0,1},{1,2},{2,3},{3,4},{4,5},{5,6},{6,7},{7,0},{8,9},{9,10},{10,1... | collective-permute-start | bytes 614408 | tf_op jit(solution)/shard_map/ppermute | solution.py:258
  156.8 7.0 %collective-permute-start.13 = (bf16[32,3200]{1,0:T(8,128)(2,1)S(1)}, bf16[32,3200]{1,0:T(8,128)(2,1)S(1)}, u32[]{:S(2)}, u32[]{:S(2)}) collective-permute-start(bf16[32,3200]{1,0:T(8,128)(2,1)S(1)} %collective-permute-done.11.refs_11_), channel_id=1, source_target_pairs={{0,7},{1,0},{2,1},{3,2},{4,3},{5,4},{6,5},{7,6},{8,15},{9,8},{10,9... | collective-permute-start | bytes 614408 | tf_op jit(solution)/shard_map/ppermute | solution.py:258
  182.8 12.9 %collective-permute-start.14 = (f32[8,512]{1,0:T(8,128)}, f32[8,512]{1,0:T(8,128)S(1)}, u32[]{:S(2)}, u32[]{:S(2)}) collective-permute-start(f32[8,512]{1,0:T(8,128)} %score.1), channel_id=1, source_target_pairs={{0,1},{1,2},{2,3},{3,4},{4,5},{5,6},{6,7},{7,0},{8,9},{9,10},{10,1... | collective-permute-start | bytes 49160 | tf_op jit(solution)/shard_map/ppermute | solution.py:258
  183.5 12.7 %collective-permute-start.15 = (f32[8,512]{1,0:T(8,128)}, f32[8,512]{1,0:T(8,128)S(1)}, u32[]{:S(2)}, u32[]{:S(2)}) collective-permute-start(f32[8,512]{1,0:T(8,128)} %score.1), channel_id=1, source_target_pairs={{0,2},{1,3},{2,4},{3,5},{4,6},{5,7},{6,0},{7,1},{8,10},{9,11},{10,... | collective-permute-start | bytes 49160 | tf_op jit(solution)/shard_map/ppermute | solution.py:258
  187.6 10.1 %collective-permute-start.16 = (f32[8,512]{1,0:T(8,128)}, f32[8,512]{1,0:T(8,128)S(1)}, u32[]{:S(2)}, u32[]{:S(2)}) collective-permute-start(f32[8,512]{1,0:T(8,128)} %score.1), channel_id=1, source_target_pairs={{0,3},{1,4},{2,5},{3,6},{4,7},{5,0},{6,1},{7,2},{8,11},{9,12},{10,... | collective-permute-start | bytes 49160 | tf_op jit(solution)/shard_map/ppermute | solution.py:258
  187.9 9.7 %collective-permute-start.17 = (f32[8,512]{1,0:T(8,128)}, f32[8,512]{1,0:T(8,128)S(1)}, u32[]{:S(2)}, u32[]{:S(2)}) collective-permute-start(f32[8,512]{1,0:T(8,128)} %score.1), channel_id=1, source_target_pairs={{0,4},{1,5},{2,6},{3,7},{4,0},{5,1},{6,2},{7,3},{8,12},{9,13},{10,... | collective-permute-start | bytes 49160 | tf_op jit(solution)/shard_map/ppermute | solution.py:258
  190.9 6.9 %collective-permute-start.18 = (f32[8,512]{1,0:T(8,128)}, f32[8,512]{1,0:T(8,128)S(1)}, u32[]{:S(2)}, u32[]{:S(2)}) collective-permute-start(f32[8,512]{1,0:T(8,128)} %score.1), channel_id=1, source_target_pairs={{0,5},{1,6},{2,7},{3,0},{4,1},{5,2},{6,3},{7,4},{8,13},{9,14},{10,... | collective-permute-start | bytes 49160 | tf_op jit(solution)/shard_map/ppermute | solution.py:258
  195.7 5.0 %collective-permute-start.19 = (f32[8,512]{1,0:T(8,128)}, f32[8,512]{1,0:T(8,128)S(1)}, u32[]{:S(2)}, u32[]{:S(2)}) collective-permute-start(f32[8,512]{1,0:T(8,128)} %score.1), channel_id=1, source_target_pairs={{0,6},{1,7},{2,0},{3,1},{4,2},{5,3},{6,4},{7,5},{8,14},{9,15},{10,... | collective-permute-start | bytes 49160 | tf_op jit(solution)/shard_map/ppermute | solution.py:258
  196.2 4.5 %collective-permute-start.20 = (f32[8,512]{1,0:T(8,128)}, f32[8,512]{1,0:T(8,128)S(1)}, u32[]{:S(2)}, u32[]{:S(2)}) collective-permute-start(f32[8,512]{1,0:T(8,128)} %score.1), channel_id=1, source_target_pairs={{0,7},{1,0},{2,1},{3,2},{4,3},{5,4},{6,5},{7,6},{8,15},{9,8},{10,9... | collective-permute-start | bytes 49160 | tf_op jit(solution)/shard_map/ppermute | solution.py:258
  (7 other events, 20.9 us)
Sparse Core Ops, SparseCore 0:
  10.6 70.2 all-gather.5
  83.5 67.5 all-gather.3
